TPU v7x, 512 devices: a whole 4x8x8 slice. The times are simulated.
512 devices in a mesh: doc: 16 (over z, core), gram: 32 (over x, y).
Axes of the slice: x: 4, y: 8, z: 8, core: 2. Of those that a mesh axis runs over, the one named last changes fastest.
Arguments:
- w_factor: bfloat16 [24576, 256], P(('doc', 'gram')), may hold values from 0.003 to 0.1
- h_factor: bfloat16 [49152, 256], P(('gram', 'doc')), may hold values from 0.003 to 0.1
- tile_counts: bfloat16 [16, 32, 24, 128, 128], P('doc', 'gram'), may hold values from 0 to 30, as said below
- tile_rows: int32 [16, 32, 24], P('doc', 'gram'), may hold values from 0 to 11, as said below
- tile_cols: int32 [16, 32, 24], P('doc', 'gram'), may hold values from 0 to 11, as said below
- tile_live: int32 [16, 32], P('doc', 'gram'), may hold values from 1 to 24, as said below
Outputs:
- w_next: bfloat16 [24576, 256], P(('doc', 'gram'))
- h_next: bfloat16 [49152, 256], P(('gram', 'doc'))
Inputs may be any that keep to these rules, and one draw needn't show every extreme that they name: `tile_rows`: within one device pair the first tile_live slots name distinct tiles; slots hold positions in every case. `tile_cols`: see tile_rows. `tile_live`: some device pair holds 24 tiles. `tile_counts`: whole numbers.
All inputs are finite; a program needn't handle non-finite values.
Results may differ from a plain program's by a relative error of at most 0.0021.
Values may be sent and summed in bfloat16 or wider, within the bound.
A program may use at most 64 MiB of HBM per device.

v0:
```python
import jax
import jax.numpy as jnp
from jax import lax
from jax.sharding import PartitionSpec as P

GROUP = 8


def group_terms(w_tiles, h_tiles, rows, cols, counts, keep):
    wt = jnp.take(w_tiles, rows, axis=0)
    ht = jnp.take(h_tiles, cols, axis=0)
    model = jnp.einsum("spk,sqk->spq", wt, ht, preferred_element_type=jnp.float32)
    ratio = (counts.astype(jnp.float32) / model * keep[:, None, None]).astype(jnp.bfloat16)
    w_part = jnp.einsum("spq,sqk->spk", ratio, ht, preferred_element_type=jnp.float32)
    h_part = jnp.einsum("spq,spk->sqk", ratio, wt, preferred_element_type=jnp.float32)
    pick_r = (rows[:, None] == jnp.arange(w_tiles.shape[0], dtype=jnp.int32)[None, :]).astype(
        jnp.float32
    )
    pick_c = (cols[:, None] == jnp.arange(h_tiles.shape[0], dtype=jnp.int32)[None, :]).astype(
        jnp.float32
    )
    add_w = jnp.einsum("st,spk->tpk", pick_r, w_part, precision=lax.Precision.HIGHEST)
    add_h = jnp.einsum("st,spk->tpk", pick_c, h_part, precision=lax.Precision.HIGHEST)
    return (add_w, add_h)


def body(w_factor, h_factor, tile_counts, tile_rows, tile_cols, tile_live):
    topics = w_factor.shape[1]
    w_block = lax.all_gather(w_factor, "gram", axis=0, tiled=True)
    h_block = lax.all_gather(h_factor, "doc", axis=0, tiled=True)
    tile_side = tile_counts.shape[3]
    w_tiles = w_block.reshape(-1, tile_side, topics)
    h_tiles = h_block.reshape(-1, tile_side, topics)
    rows = tile_rows[0, 0]
    cols = tile_cols[0, 0]
    counts = tile_counts[0, 0]
    live = tile_live[0, 0]
    slots = rows.shape[0]
    width = GROUP
    start = (jnp.zeros(w_tiles.shape, jnp.float32), jnp.zeros(h_tiles.shape, jnp.float32))
    steps = slots // width
    marks = (jnp.arange(slots, dtype=jnp.int32) < live).astype(jnp.float32)

    def visit(carry, pieces):
        part_rows, part_cols, part_counts, part_keep = pieces
        add_w, add_h = group_terms(w_tiles, h_tiles, part_rows, part_cols, part_counts, part_keep)
        return ((carry[0] + add_w, carry[1] + add_h), None)

    pieces = (
        rows.reshape(steps, width),
        cols.reshape(steps, width),
        counts.reshape(steps, width, tile_side, tile_side),
        marks.reshape(steps, width),
    )
    (w_numer, h_numer), _ = lax.scan(visit, start, pieces)
    flat_w = w_numer.reshape(-1, topics)
    flat_h = h_numer.reshape(-1, topics)
    w_rows = w_factor.shape[0]
    h_rows = h_factor.shape[0]
    summed_w = lax.psum(flat_w, "gram")
    share_w = lax.dynamic_slice_in_dim(summed_w, lax.axis_index("gram") * w_rows, w_rows, 0)
    summed_h = lax.psum(flat_h, "doc")
    share_h = lax.dynamic_slice_in_dim(summed_h, lax.axis_index("doc") * h_rows, h_rows, 0)
    h_sums = jnp.sum(h_factor.astype(jnp.float32), axis=0)
    w_sums = jnp.sum(w_factor.astype(jnp.float32), axis=0)
    w_denom, h_denom = lax.psum((h_sums, w_sums), ("doc", "gram"))
    w_next = (w_factor.astype(jnp.float32) * share_w / w_denom).astype(jnp.bfloat16)
    h_next = (h_factor.astype(jnp.float32) * share_h / h_denom).astype(jnp.bfloat16)
    return (w_next, h_next)


def solution(mesh):
    in_specs = (
        P(("doc", "gram"), None),
        P(("gram", "doc"), None),
        P("doc", "gram", None, None, None),
        P("doc", "gram", None),
        P("doc", "gram", None),
        P("doc", "gram"),
    )
    out_specs = (P(("doc", "gram"), None), P(("gram", "doc"), None))
    return jax.shard_map(body, mesh=mesh, in_specs=in_specs, out_specs=out_specs, check_vma=False)
```

profile of v0, /device:TPU:64, one launch (start us, length us, event | category | flops | bytes accessed | tf_op | source)
XLA Modules:
  0.0 419.8 jit_solution(2480098275050584792)
XLA Ops:
  7.2 0.0 all-reduce.6.cloned.1.call-start
  7.2 0.5 broadcast.73
  7.7 1.3 reduce.6
  9.1 0.1 reshape_squeeze.9
  9.1 50.8 %all_gather.6 = bf16[1536,256]{1,0:T(8,128)(2,1)S(1)} all-gather(bf16[48,256]{1,0:T(8,128)(2,1)} %param.10), channel_id=1, replica_groups=mesh['doc'=16,'gram'=32] {'gram'}, dimensions={0}, use_global_device_ids=true | all-gather | bytes 811008 | tf_op jit(solution)/shard_map/all_gather | solution.py:29
  60.0 1.3 reduce.7
  61.3 0.1 reshape_squeeze.11
  61.4 23.9 %all_gather.7 = bf16[1536,256]{1,0:T(8,128)(2,1)} all-gather(bf16[96,256]{1,0:T(8,128)(2,1)} %param.11), channel_id=1, replica_groups=mesh['doc'=16,'gram'=32] {'doc'}, dimensions={0}, use_global_device_ids=true | all-gather | bytes 835584 | tf_op jit(solution)/shard_map/all_gather | solution.py:30
  85.9 38.7 %while.13 = (s32[]{:T(128)}, f32[12,128,256]{2,0,1:T(8,128)S(1)}, f32[12,128,256]{2,0,1:T(8,128)}, s32[3,8]{1,0:T(4,128)S(1)}, bf16[3,8,128,128]{3,2,1,0:T(8,128...) while((s32[]{:T(128)}, f32[12,128,256]{2,0,1:T(8,128)S(1)}, ...), condition=%wide.region_1.3_spmd.clone, body=%wide.region_0.2_spmd.clone.sunk | while | flops 279972160 | bytes 40903584 | solution.py:55
  86.0 0.6 gather_fusion
  86.6 0.2 copy-done.5
  86.8 1.7 gather_fusion.1
  88.6 0.8 copy-done.4
  89.3 1.3 fusion.44
  90.7 1.4 fusion.45
  92.1 2.5 select_add_fusion.4
  94.6 0.4 fusion.46
  95.0 2.5 select_add_fusion.5
  97.5 1.3 copy-done.1
  98.9 0.6 gather_fusion
  99.5 0.2 copy-done.5
  99.7 1.7 gather_fusion.1
  101.5 0.8 copy-done.4
  102.2 1.3 fusion.44
  103.6 1.4 fusion.45
  105.0 2.5 select_add_fusion.4
  107.5 0.4 fusion.46
  107.9 2.5 select_add_fusion.5
  110.4 1.3 copy-done.1
  111.8 0.6 gather_fusion
  112.4 0.2 copy-done.5
  112.6 1.7 gather_fusion.1
  114.4 0.8 copy-done.4
  115.1 1.3 fusion.44
  116.5 1.4 fusion.45
  117.9 2.5 select_add_fusion.4
  120.4 0.4 fusion.46
  120.8 2.5 select_add_fusion.5
  123.3 1.3 copy-done.1
  124.6 3.7 copy.9
  128.3 0.0 all-reduce.6.cloned.1.call-update
  128.3 0.0 all-reduce.4.cloned.1.call-start
  128.4 2.1 copy.8
  130.6 96.5 %all-reduce = (f32[256]{0:T(256)S(1)}, f32[256]{0:T(256)S(1)}) all-reduce(f32[256]{0:T(256)S(1)} %convert_reduce_fusion, f32[256]{0:T(256)S(1)} %convert_reduce_fusion.1), channel_id=1, replica_groups=mesh['doc'=16,'gram'=32] {'doc','gram'}, use_global_device_ids=true, to_apply=%region_4.6 | all-reduce | flops 512 | bytes 4096 | tf_op jit(solution)/shard_map/psum | solution.py:66
  227.1 15.2 %all-reduce.6.cloned.1.call-done = f32[1536,256]{1,0:T(8,128)} async-done(((f32[1536,256]{1,0:T(8,128)}), f32[1536,256]{1,0:T(8,128)}) %all-reduce.6.cloned.1.call-update) | async-done | bytes 1572880 | tf_op jit(solution)/shard_map/psum | solution.py:62
  242.3 1.5 fusion.19
  243.8 167.7 %all-reduce.4.cloned.1.call-done = f32[1536,256]{1,0:T(8,128)} async-done(((f32[1536,256]{1,0:T(8,128)}), f32[1536,256]{1,0:T(8,128)}) %all-reduce.4.cloned.1.call-update) | async-done | bytes 1572880 | tf_op jit(solution)/shard_map/psum | solution.py:60
  411.6 1.4 fusion.21
  (61 shorter events, 0.3 us)
Async XLA Ops:
  7.2 235.2 %all-reduce.6.cloned.1.call-start = ((), (), s32[]{:S(2)}) async-start(), calls=%async_computation.1 | async-start | bytes 3145728 | tf_op jit(solution)/shard_map/psum | solution.py:62
  85.9 0.9 copy-start.5
  86.6 2.0 copy-start.2
  88.5 0.8 copy-start.4
  92.1 2.5 copy-start.3
  92.1 2.9 copy-start
  95.0 3.8 copy-start.6
  97.5 1.4 copy-start.1
  98.8 0.9 copy-start.5
  99.5 2.0 copy-start.2
  101.4 0.8 copy-start.4
  105.0 2.5 copy-start.3
  105.0 2.9 copy-start
  107.9 3.8 copy-start.6
  110.4 1.4 copy-start.1
  111.7 0.9 copy-start.5
  112.4 2.0 copy-start.2
  114.3 0.8 copy-start.4
  117.9 2.5 copy-start.3
  117.9 2.9 copy-start
  120.8 3.8 copy-start.6
  123.3 1.4 copy-start.1
  128.3 283.3 %all-reduce.4.cloned.1.call-start = ((), (), s32[]{:S(2)}) async-start(), calls=%async_computation | async-start | bytes 3145728 | tf_op jit(solution)/shard_map/psum | solution.py:60
  128.4 2.2 copy-start.8
  128.4 2.2 copy-start.7
Sparse Core Ops, SparseCore 0:
  128.4 113.8 all-reduce.5
  245.7 165.8 all-reduce.3
where the time goes:
time: 421 us; the launch traced here: 420 us
  waiting for transfers between devices  183 us (43%)
  blocking collectives  171 us (41%)
  matrix products  24.2 us (6%)
  local copies, waits for them, and re-layouts  20.4 us (5%)
  between operations  14.8 us (4%)
  other arithmetic  5.76 us (1%)
    psum x1, waiting for transfers between devices, body(): summed_w = lax.psum(flat_w, 'gram')  168 us
    psum x1, blocking collectives, body(): w_denom, h_denom = lax.psum((h_sums, w_sums), ('doc', 'gram'))  96.5 us
    all_gather x1, blocking collectives, body(): w_block = lax.all_gather(w_factor, 'gram', axis=0, tiled=True)  50.8 us
    all_gather x1, blocking collectives, body(): h_block = lax.all_gather(h_factor, 'doc', axis=0, tiled=True)  23.9 us
    psum x1, waiting for transfers between devices, body(): summed_h = lax.psum(flat_h, 'doc')  15.2 us
  transfers between devices with their start and end apart: 2, of which 2 were waited for; matrix products, arithmetic and copies ran while one was open for 1% of the time, Pallas kernels for 0%

commit v1 on v0

--- a/solution.py
+++ b/solution.py
@@ -1,9 +1,22 @@
+import functools
 import jax
 import jax.numpy as jnp
 from jax import lax
 from jax.sharding import PartitionSpec as P
 
 GROUP = 8
+
+
+def _build_space(base_x, along_axis):
+    world = lax.psum(1, along_axis)
+    frame_out = lambda fresh: [(tick, tick ^ fresh) for tick in range(world)]
+    a_next = base_x
+    for c in range(world.bit_length() - 1):
+        a_next = a_next + lax.ppermute(a_next, along_axis, frame_out(1 << c))
+    return a_next
+
+
+_mark_series_all = functools.partial(_build_space, along_axis="gram")
 
 
 def group_terms(w_tiles, h_tiles, rows, cols, counts, keep):
@@ -57,7 +70,7 @@
     flat_h = h_numer.reshape(-1, topics)
     w_rows = w_factor.shape[0]
     h_rows = h_factor.shape[0]
-    summed_w = lax.psum(flat_w, "gram")
+    summed_w = _mark_series_all(flat_w)
     share_w = lax.dynamic_slice_in_dim(summed_w, lax.axis_index("gram") * w_rows, w_rows, 0)
     summed_h = lax.psum(flat_h, "doc")
     share_h = lax.dynamic_slice_in_dim(summed_h, lax.axis_index("doc") * h_rows, h_rows, 0)

time: 421 us -> 485 us (1.15)
  the two profiles are of different devices: /device:TPU:64 before, /device:TPU:1 now
where the time goes in v1:
time: 485 us; the launch traced here: 484 us
  waiting for transfers between devices  226 us (47%)
  blocking collectives  175 us (36%)
  matrix products  27.1 us (6%)
  starting transfers between devices  20 us (4%)
  between operations  14.8 us (3%)
  local copies, waits for them, and re-layouts  13.6 us (3%)
  other arithmetic  7.73 us (2%)
    ppermute x5, waiting for transfers between devices, _build_space(): a_next = a_next + lax.ppermute(a_next, along_axis, frame_out(1 << c))  207 us
    psum x1, blocking collectives, body(): w_denom, h_denom = lax.psum((h_sums, w_sums), ('doc', 'gram'))  95.5 us
    all_gather x1, blocking collectives, body(): w_block = lax.all_gather(w_factor, 'gram', axis=0, tiled=True)  40.1 us
    all_gather x1, blocking collectives, body(): h_block = lax.all_gather(h_factor, 'doc', axis=0, tiled=True)  39.1 us
    ppermute x5, starting transfers between devices, _build_space(): a_next = a_next + lax.ppermute(a_next, along_axis, frame_out(1 << c))  20 us
    psum x1, waiting for transfers between devices, body(): summed_h = lax.psum(flat_h, 'doc')  18.4 us
    dot_general x3, matrix products, group_terms(): jnp.einsum('st,spk->tpk', pick_c, h_part, precision=lax.Precision.HIGHEST)  10.3 us
  transfers between devices with their start and end apart: 6, of which 5 were waited for; matrix products, arithmetic and copies ran while one was open for 1% of the time, Pallas kernels for 0%

profile of v1, /device:TPU:1, one launch (start us, length us, event | category | flops | bytes accessed | tf_op | source)
XLA Modules:
  0.0 484.1 jit_solution(17755318739330288574)
XLA Ops:
  7.2 0.5 broadcast.73
  7.7 1.3 reduce.7
  9.1 1.3 reduce.6
  10.5 40.1 %all_gather.6 = bf16[1536,256]{1,0:T(8,128)(2,1)S(1)} all-gather(bf16[48,256]{1,0:T(8,128)(2,1)} %param.10), channel_id=1, replica_groups=mesh['doc'=16,'gram'=32] {'gram'}, dimensions={0}, use_global_device_ids=true | all-gather | bytes 811008 | tf_op jit(solution)/shard_map/all_gather | solution.py:42
  50.6 39.1 %all_gather.7 = bf16[1536,256]{1,0:T(8,128)(2,1)} all-gather(bf16[96,256]{1,0:T(8,128)(2,1)} %param.11), channel_id=1, replica_groups=mesh['doc'=16,'gram'=32] {'doc'}, dimensions={0}, use_global_device_ids=true | all-gather | bytes 835584 | tf_op jit(solution)/shard_map/all_gather | solution.py:43
  90.3 37.5 %while.13 = (s32[]{:T(128)}, f32[12,128,256]{2,0,1:T(8,128)S(1)}, f32[12,128,256]{2,0,1:T(8,128)}, s32[3,8]{1,0:T(4,128)S(1)}, bf16[3,8,128,128]{3,2,1,0:T(8,128...) while((s32[]{:T(128)}, f32[12,128,256]{2,0,1:T(8,128)S(1)}, ...), condition=%wide.region_1.3_spmd.clone, body=%wide.region_0.2_spmd.clone.sunk | while | flops 279972160 | bytes 28320608 | solution.py:68
  90.4 0.6 gather_fusion
  91.2 1.7 gather_fusion.1
  93.0 0.8 copy-done.1
  93.7 1.3 fusion.44
  95.1 1.4 fusion.46
  96.5 2.6 select_add_fusion.5
  99.1 0.4 fusion.45
  99.5 2.5 select_add_fusion.4
  102.1 0.6 gather_fusion
  102.9 1.7 gather_fusion.1
  104.6 0.8 copy-done.1
  105.4 1.3 fusion.44
  106.8 1.4 fusion.46
  108.2 3.9 select_add_fusion.5
  112.0 0.4 fusion.45
  112.4 2.5 select_add_fusion.4
  115.0 0.6 gather_fusion
  115.8 1.7 gather_fusion.1
  117.6 0.8 copy-done.1
  118.3 1.3 fusion.44
  119.7 1.4 fusion.46
  121.1 3.9 select_add_fusion.5
  125.0 0.4 fusion.45
  125.3 2.5 select_add_fusion.4
  127.8 0.9 copy.8
  128.8 2.4 collective-permute-start
  131.2 35.3 %collective-permute-done = f32[1536,256]{1,0:T(8,128)S(1)} collective-permute-done((f32[1536,256]{1,0:T(8,128)S(1)}, f32[1536,256]{1,0:T(8,128)S(1)}, u32[]{:S(2)}, u32[]{:S(2)}) %collective-permute-start) | collective-permute-done | bytes 1572896 | tf_op jit(solution)/shard_map/ppermute | solution.py:15
  166.6 3.6 collective-permute-start.1
  170.3 68.9 %collective-permute-done.1 = f32[1536,256]{1,0:T(8,128)S(1)} collective-permute-done((f32[1536,256]{1,0:T(8,128)S(1)}, f32[1536,256]{1,0:T(8,128)S(1)}, u32[]{:S(2)}, u32[]{:S(2)}) %collective-permute-start.1) | collective-permute-done | bytes 1572896 | tf_op jit(solution)/shard_map/ppermute | solution.py:15
  239.2 0.2 add.41
  239.5 6.0 %collective-permute-start.2 = (f32[1536,256]{1,0:T(8,128)S(1)}, f32[1536,256]{1,0:T(8,128)S(1)}, u32[]{:S(2)}, u32[]{:S(2)}) collective-permute-start(f32[1536,256]{1,0:T(8,128)S(1)} %add.41), channel_id=1, source_target_pairs={{0,4},{1,5},{2,6},{3,7},{4,0},{5,1},{6,2},{7,3},{8,12},{9,13},{10,... | collective-permute-start | bytes 4718600 | tf_op jit(solution)/shard_map/ppermute | solution.py:15
  245.4 69.1 %collective-permute-done.2 = f32[1536,256]{1,0:T(8,128)S(1)} collective-permute-done((f32[1536,256]{1,0:T(8,128)S(1)}, f32[1536,256]{1,0:T(8,128)S(1)}, u32[]{:S(2)}, u32[]{:S(2)}) %collective-permute-start.2) | collective-permute-done | bytes 1572896 | tf_op jit(solution)/shard_map/ppermute | solution.py:15
  314.6 0.2 add.42
  314.8 2.5 collective-permute-start.3
  317.3 34.0 %collective-permute-done.3 = f32[1536,256]{1,0:T(8,128)S(1)} collective-permute-done((f32[1536,256]{1,0:T(8,128)S(1)}, f32[1536,256]{1,0:T(8,128)S(1)}, u32[]{:S(2)}, u32[]{:S(2)}) %collective-permute-start.3) | collective-permute-done | bytes 1572896 | tf_op jit(solution)/shard_map/ppermute | solution.py:15
  351.3 1.3 add.43
  352.6 5.5 %collective-permute-start.4 = (f32[1536,256]{1,0:T(8,128)}, f32[1536,256]{1,0:T(8,128)}, u32[]{:S(2)}, u32[]{:S(2)}) collective-permute-start(f32[1536,256]{1,0:T(8,128)} %add.43), channel_id=1, source_target_pairs={{0,16},{1,17},{2,18},{3,19},{4,20},{5,21},{6,22},{7,23},{8,24},{9,... | collective-permute-start | bytes 4718600 | tf_op jit(solution)/shard_map/ppermute | solution.py:15
  358.1 2.1 copy.9
  360.4 95.5 %all-reduce = (f32[256]{0:T(256)S(1)}, f32[256]{0:T(256)S(1)}) all-reduce(f32[256]{0:T(256)S(1)} %convert_reduce_fusion, f32[256]{0:T(256)S(1)} %convert_reduce_fusion.1), channel_id=1, replica_groups=mesh['doc'=16,'gram'=32] {'doc','gram'}, use_global_device_ids=true, to_apply=%region_3.5 | all-reduce | flops 512 | bytes 4096 | tf_op jit(solution)/shard_map/psum | solution.py:79
  455.9 18.4 %all-reduce.3.cloned.1.call-done = f32[1536,256]{1,0:T(8,128)} async-done(((f32[1536,256]{1,0:T(8,128)}), f32[1536,256]{1,0:T(8,128)}) %all-reduce.3.cloned.1.call-update) | async-done | bytes 1572880 | tf_op jit(solution)/shard_map/psum | solution.py:75
  474.3 1.5 fusion.19
  475.8 1.4 fusion.21
  (62 shorter events, 1.3 us)
Async XLA Ops:
  7.2 467.1 %all-reduce.3.cloned.1.call-start = ((), (), s32[]{:S(2)}) async-start(), calls=%async_computation | async-start | bytes 3145728 | tf_op jit(solution)/shard_map/psum | solution.py:75
  90.3 0.9 copy-start.4
  91.0 2.0 copy-start.3
  92.9 0.8 copy-start.1
  96.5 2.6 copy-start.2
  99.5 2.5 copy-start.5
  102.0 0.9 copy-start.4
  102.7 2.0 copy-start.3
  104.6 0.8 copy-start.1
  108.2 3.9 copy-start.2
  112.4 2.5 copy-start.5
  114.9 0.9 copy-start.4
  115.6 2.0 copy-start.3
  117.5 0.8 copy-start.1
  121.1 3.9 copy-start.2
  125.3 2.5 copy-start.5
  128.8 37.7 %collective-permute-start = (f32[1536,256]{1,0:T(8,128)S(1)}, f32[1536,256]{1,0:T(8,128)S(1)}, u32[]{:S(2)}, u32[]{:S(2)}) collective-permute-start(f32[1536,256]{1,0:T(8,128)S(1)} %bitcast.42), channel_id=1, source_target_pairs={{0,1},{1,0},{2,3},{3,2},{4,5},{5,4},{6,7},{7,6},{8,9},{9,8},{10,11... | collective-permute-start | bytes 4718600 | tf_op jit(solution)/shard_map/ppermute | solution.py:15
  166.6 72.6 %collective-permute-start.1 = (f32[1536,256]{1,0:T(8,128)S(1)}, f32[1536,256]{1,0:T(8,128)S(1)}, u32[]{:S(2)}, u32[]{:S(2)}) collective-permute-start(f32[1536,256]{1,0:T(8,128)S(1)} %bitcast_add_fusion), channel_id=1, source_target_pairs={{0,2},{1,3},{2,0},{3,1},{4,6},{5,7},{6,4},{7,5},{8,10},{9,11},{10,... | collective-permute-start | bytes 4718600 | tf_op jit(solution)/shard_map/ppermute | solution.py:15
  239.5 75.1 %collective-permute-start.2 = (f32[1536,256]{1,0:T(8,128)S(1)}, f32[1536,256]{1,0:T(8,128)S(1)}, u32[]{:S(2)}, u32[]{:S(2)}) collective-permute-start(f32[1536,256]{1,0:T(8,128)S(1)} %add.41), channel_id=1, source_target_pairs={{0,4},{1,5},{2,6},{3,7},{4,0},{5,1},{6,2},{7,3},{8,12},{9,13},{10,... | collective-permute-start | bytes 4718600 | tf_op jit(solution)/shard_map/ppermute | solution.py:15
  314.8 43.4 %copy-start = (f32[12,128,256]{2,0,1:T(8,128)S(1)}, f32[12,128,256]{2,0,1:T(8,128)}, u32[]{:S(2)}) copy-start(f32[12,128,256]{2,0,1:T(8,128)} %get-tuple-element.52) | copy-start | bytes 4718596
  314.8 36.5 %collective-permute-start.3 = (f32[1536,256]{1,0:T(8,128)S(1)}, f32[1536,256]{1,0:T(8,128)S(1)}, u32[]{:S(2)}, u32[]{:S(2)}) collective-permute-start(f32[1536,256]{1,0:T(8,128)S(1)} %add.42), channel_id=1, source_target_pairs={{0,8},{1,9},{2,10},{3,11},{4,12},{5,13},{6,14},{7,15},{8,0},{9,1},... | collective-permute-start | bytes 4718600 | tf_op jit(solution)/shard_map/ppermute | solution.py:15
  352.6 123.2 %collective-permute-start.4 = (f32[1536,256]{1,0:T(8,128)}, f32[1536,256]{1,0:T(8,128)}, u32[]{:S(2)}, u32[]{:S(2)}) collective-permute-start(f32[1536,256]{1,0:T(8,128)} %add.43), channel_id=1, source_target_pairs={{0,16},{1,17},{2,18},{3,19},{4,20},{5,21},{6,22},{7,23},{8,24},{9,... | collective-permute-start | bytes 4718600 | tf_op jit(solution)/shard_map/ppermute | solution.py:15
  358.1 2.2 copy-start.7
  358.1 2.2 copy-start.6
Sparse Core Ops, SparseCore 0:
  360.4 113.8 all-reduce.2

commit v2 on v0

--- a/solution.py
+++ b/solution.py
@@ -63,7 +63,7 @@
     share_h = lax.dynamic_slice_in_dim(summed_h, lax.axis_index("doc") * h_rows, h_rows, 0)
     h_sums = jnp.sum(h_factor.astype(jnp.float32), axis=0)
     w_sums = jnp.sum(w_factor.astype(jnp.float32), axis=0)
-    w_denom, h_denom = lax.psum((h_sums, w_sums), ("doc", "gram"))
+    w_denom, h_denom = lax.psum(lax.psum((h_sums, w_sums), axis_name="doc"), axis_name="gram")
     w_next = (w_factor.astype(jnp.float32) * share_w / w_denom).astype(jnp.bfloat16)
     h_next = (h_factor.astype(jnp.float32) * share_h / h_denom).astype(jnp.bfloat16)
     return (w_next, h_next)

time: 421 us -> 421 us (level)
    psum x1 -> x2, blocking collectives: 96.5 us -> 95.4 us  [the longest x1 72.3 us: body(): lax.psum(lax.psum((h_sums, w_sums), axis_name='doc'), axis_name='gram')]
where the time goes in v2:
time: 421 us; the launch traced here: 420 us
  waiting for transfers between devices  184 us (44%)
  blocking collectives  170 us (40%)
  matrix products  24.2 us (6%)
  local copies, waits for them, and re-layouts  20.4 us (5%)
  between operations  14.8 us (4%)
  other arithmetic  5.75 us (1%)
    psum x1, waiting for transfers between devices, body(): summed_w = lax.psum(flat_w, 'gram')  168 us
    psum x1, blocking collectives, body(): lax.psum(lax.psum((h_sums, w_sums), axis_name='doc'), axis_name='gram')  72.3 us
    all_gather x1, blocking collectives, body(): w_block = lax.all_gather(w_factor, 'gram', axis=0, tiled=True)  50.8 us
    all_gather x1, blocking collectives, body(): h_block = lax.all_gather(h_factor, 'doc', axis=0, tiled=True)  23.9 us
    psum x1, blocking collectives, body(): lax.psum((h_sums, w_sums), axis_name='doc')  23.1 us
    psum x1, waiting for transfers between devices, body(): summed_h = lax.psum(flat_h, 'doc')  16.6 us
  transfers between devices with their start and end apart: 2, of which 2 were waited for; matrix products, arithmetic and copies ran while one was open for 1% of the time, Pallas kernels for 0%

profile of v2, /device:TPU:64, one launch (start us, length us, event | category | flops | bytes accessed | tf_op | source)
XLA Modules:
  0.0 420.0 jit_solution(14159535712012497459)
XLA Ops:
  7.2 0.0 all-reduce.7.cloned.1.call-start
  7.2 0.5 broadcast.73
  7.7 1.3 reduce.6
  9.1 0.1 reshape_squeeze.9
  9.1 50.8 %all_gather.6 = bf16[1536,256]{1,0:T(8,128)(2,1)S(1)} all-gather(bf16[48,256]{1,0:T(8,128)(2,1)} %param.10), channel_id=1, replica_groups=mesh['doc'=16,'gram'=32] {'gram'}, dimensions={0}, use_global_device_ids=true | all-gather | bytes 811008 | tf_op jit(solution)/shard_map/all_gather | solution.py:29
  60.0 1.3 reduce.7
  61.3 0.1 reshape_squeeze.11
  61.4 23.9 %all_gather.7 = bf16[1536,256]{1,0:T(8,128)(2,1)} all-gather(bf16[96,256]{1,0:T(8,128)(2,1)} %param.11), channel_id=1, replica_groups=mesh['doc'=16,'gram'=32] {'doc'}, dimensions={0}, use_global_device_ids=true | all-gather | bytes 835584 | tf_op jit(solution)/shard_map/all_gather | solution.py:30
  85.9 38.7 %while.13 = (s32[]{:T(128)}, f32[12,128,256]{2,0,1:T(8,128)S(1)}, f32[12,128,256]{2,0,1:T(8,128)}, s32[3,8]{1,0:T(4,128)S(1)}, bf16[3,8,128,128]{3,2,1,0:T(8,128...) while((s32[]{:T(128)}, f32[12,128,256]{2,0,1:T(8,128)S(1)}, ...), condition=%wide.region_1.3_spmd.clone, body=%wide.region_0.2_spmd.clone.sunk | while | flops 279972160 | bytes 40903584 | solution.py:55
  86.0 0.6 gather_fusion
  86.6 0.2 copy-done.5
  86.8 1.7 gather_fusion.1
  88.6 0.8 copy-done.4
  89.3 1.3 fusion.44
  90.7 1.4 fusion.45
  92.1 2.5 select_add_fusion.4
  94.6 0.4 fusion.46
  95.0 2.5 select_add_fusion.5
  97.5 1.3 copy-done.1
  98.9 0.6 gather_fusion
  99.5 0.2 copy-done.5
  99.7 1.7 gather_fusion.1
  101.5 0.8 copy-done.4
  102.2 1.3 fusion.44
  103.6 1.4 fusion.45
  105.0 2.5 select_add_fusion.4
  107.5 0.4 fusion.46
  107.9 2.5 select_add_fusion.5
  110.4 1.3 copy-done.1
  111.8 0.6 gather_fusion
  112.4 0.2 copy-done.5
  112.6 1.7 gather_fusion.1
  114.4 0.8 copy-done.4
  115.1 1.3 fusion.44
  116.5 1.4 fusion.45
  117.9 2.5 select_add_fusion.4
  120.4 0.4 fusion.46
  120.8 2.5 select_add_fusion.5
  123.3 1.3 copy-done.1
  124.6 3.7 copy.9
  128.3 0.0 all-reduce.5.cloned.1.call-start
  128.4 2.1 copy.8
  130.6 23.1 %all-reduce.1 = (f32[256]{0:T(256)S(1)}, f32[256]{0:T(256)S(1)}) all-reduce(f32[256]{0:T(256)S(1)} %convert_reduce_fusion, f32[256]{0:T(256)S(1)} %convert_reduce_fusion.1), channel_id=1, replica_groups=mesh['doc'=16,'gram'=32] {'doc'}, use_global_device_ids=true, to_apply=%region_4.6 | all-reduce | flops 512 | bytes 4096 | tf_op jit(solution)/shard_map/psum | solution.py:66
  153.8 72.3 %all-reduce = (f32[256]{0:T(256)S(1)}, f32[256]{0:T(256)S(1)}) all-reduce(f32[256]{0:T(256)S(1)} %get-tuple-element.103, f32[256]{0:T(256)S(1)} %get-tuple-element.104), channel_id=1, replica_groups=mesh['doc'=16,'gram'=32] {'gram'}, use_global_device_ids=true, to_apply=%region_5.7 | all-reduce | flops 512 | bytes 4096 | tf_op jit(solution)/shard_map/psum | solution.py:66
  226.0 16.6 %all-reduce.7.cloned.1.call-done = f32[1536,256]{1,0:T(8,128)} async-done(((f32[1536,256]{1,0:T(8,128)}), f32[1536,256]{1,0:T(8,128)}) %all-reduce.7.cloned.1.call-update) | async-done | bytes 1572880 | tf_op jit(solution)/shard_map/psum | solution.py:62
  242.7 1.5 fusion.19
  244.2 167.6 %all-reduce.5.cloned.1.call-done = f32[1536,256]{1,0:T(8,128)} async-done(((f32[1536,256]{1,0:T(8,128)}), f32[1536,256]{1,0:T(8,128)}) %all-reduce.5.cloned.1.call-update) | async-done | bytes 1572880 | tf_op jit(solution)/shard_map/psum | solution.py:60
  411.8 1.4 fusion.21
  (62 shorter events, 0.3 us)
Async XLA Ops:
  7.2 235.5 %all-reduce.7.cloned.1.call-start = ((), (), s32[]{:S(2)}) async-start(), calls=%async_computation.1 | async-start | bytes 3145728 | tf_op jit(solution)/shard_map/psum | solution.py:62
  85.9 0.9 copy-start.5
  86.6 2.0 copy-start.2
  88.5 0.8 copy-start.4
  92.1 2.5 copy-start.3
  92.1 2.9 copy-start
  95.0 3.8 copy-start.6
  97.5 1.4 copy-start.1
  98.8 0.9 copy-start.5
  99.5 2.0 copy-start.2
  101.4 0.8 copy-start.4
  105.0 2.5 copy-start.3
  105.0 2.9 copy-start
  107.9 3.8 copy-start.6
  110.4 1.4 copy-start.1
  111.7 0.9 copy-start.5
  112.4 2.0 copy-start.2
  114.3 0.8 copy-start.4
  117.9 2.5 copy-start.3
  117.9 2.9 copy-start
  120.8 3.8 copy-start.6
  123.3 1.4 copy-start.1
  128.3 283.4 %all-reduce.5.cloned.1.call-start = ((), (), s32[]{:S(2)}) async-start(), calls=%async_computation | async-start | bytes 3145728 | tf_op jit(solution)/shard_map/psum | solution.py:60
  128.4 2.2 copy-start.8
  128.4 2.2 copy-start.7
Sparse Core Ops, SparseCore 0:
  128.4 114.1 all-reduce.6
  246.1 165.6 all-reduce.4
